TPU v7x, 32 devices: a whole 2x2x4 slice. The times are simulated.
32 devices in a mesh: rep: 4 (over y, core), tp: 8 (over z, x).
Axes of the slice: x: 2, y: 2, z: 4, core: 2. Of those that a mesh axis runs over, the one named last changes fastest.
Arguments:
- inputs: bfloat16 [16384, 1024], P(('rep', 'tp')), may hold values from -6 to 6
- cotangent: bfloat16 [16384, 8192], P('rep', 'tp'), may hold values from -1 to 1
- master: float32 [1024, 8192], P('rep', 'tp'), may hold values from -6 to 6
- moment: float32 [1024, 8192], P('rep', 'tp'), may hold values from -6 to 6
- second: float32 [1024, 8192], P('rep', 'tp'), may hold values from 0.5 to 4
Outputs:
- combined: float32 [1024, 8192], P('rep', 'tp')
- moment_new: float32 [1024, 8192], P('rep', 'tp')
- second_new: float32 [1024, 8192], P('rep', 'tp')
- master_new: float32 [1024, 8192], P('rep', 'tp')
- weights: bfloat16 [1024, 8192], P(None, 'tp')
All inputs are finite; a program needn't handle non-finite values.
Results may differ from a plain program's by a relative error of at most 0.001.
Values may be sent and summed in bfloat16 or wider, within the bound.
A program may use at most 64 MiB of HBM per device.

v0:
```python
import jax
import jax.numpy as jnp
from jax import lax
from jax.sharding import PartitionSpec as P

EPS_SUM = 1e-06
BETA_ONE = 0.9
BETA_TWO = 0.999
LEARN = 0.01
CORRECT_ONE = 1.0 - 0.9**50
CORRECT_TWO = 1.0 - 0.999**50


def from_partner(value, axis, stride):
    return lax.ppermute(value, axis, [(i, i ^ 1 << stride) for i in range(lax.axis_size(axis))])


def trade_halves(sent_rows, distance_bit):
    return from_partner(sent_rows, "rep", distance_bit)


def combine_level(kept_rows, received, is_upper, distance_bit, levels):
    lower_part = jnp.where(is_upper, received, kept_rows)
    upper_part = jnp.where(is_upper, kept_rows, received)
    partial_value = jnp.stack(
        [
            jnp.sum(lower_part * lower_part),
            jnp.sum(upper_part * upper_part),
            jnp.sum(lower_part * upper_part),
        ]
    )
    for inner_bit in range(distance_bit, levels):
        partial_value = partial_value + from_partner(partial_value, "rep", inner_bit)
    partial_value = lax.psum(partial_value, "tp")
    low_low = partial_value[0]
    high_high = partial_value[1]
    cross_term = partial_value[2]
    lower_coef = 1.0 - cross_term / (2.0 * (low_low + EPS_SUM))
    upper_coef = 1.0 - cross_term / (2.0 * (high_high + EPS_SUM))
    return lower_coef * lower_part + upper_coef * upper_part


def per_device(inputs, cotangent, master, moment, second):
    replicas = lax.axis_size("rep")
    levels = replicas.bit_length() - 1
    my_index = lax.axis_index("rep")
    top_bit = levels - 1
    gathered_rows = lax.all_gather(inputs, "tp", axis=0, tiled=True)
    is_upper = my_index >> top_bit & 1 == 1
    half_width = gathered_rows.shape[1] // 2
    sent_start = jnp.where(is_upper, 0, half_width).astype(jnp.int32)
    kept_start = half_width - sent_start
    sent_columns = lax.dynamic_slice_in_dim(gathered_rows, sent_start, half_width, 1)
    sent_rows = lax.dot_general(
        sent_columns, cotangent, (((0,), (0,)), ((), ())), preferred_element_type=jnp.float32
    )
    received = trade_halves(sent_rows, top_bit)
    kept_columns = lax.dynamic_slice_in_dim(gathered_rows, kept_start, half_width, 1)
    kept_rows = lax.dot_general(
        kept_columns, cotangent, (((0,), (0,)), ((), ())), preferred_element_type=jnp.float32
    )
    segment = combine_level(kept_rows, received, is_upper, top_bit, levels)
    first_level = 1
    for level_index in range(first_level, levels):
        distance_bit = levels - 1 - level_index
        is_upper = my_index >> distance_bit & 1 == 1
        half_rows = segment.shape[0] // 2
        front_half = segment[:half_rows]
        back_half = segment[half_rows:]
        kept_rows = jnp.where(is_upper, back_half, front_half)
        sent_rows = jnp.where(is_upper, front_half, back_half)
        received = trade_halves(sent_rows, distance_bit)
        segment = combine_level(kept_rows, received, is_upper, distance_bit, levels)
    moment_new = BETA_ONE * moment + (1.0 - BETA_ONE) * segment
    second_new = BETA_TWO * second + (1.0 - BETA_TWO) * segment * segment
    master_new = master - LEARN * (moment_new / CORRECT_ONE) / (
        jnp.sqrt(second_new / CORRECT_TWO) + 1e-08
    )
    weights = lax.all_gather(master_new.astype(jnp.bfloat16), "rep", axis=0, tiled=True)
    return (segment, moment_new, second_new, master_new, weights)


def solution(mesh):
    return jax.shard_map(
        per_device,
        mesh=mesh,
        in_specs=(
            P(("rep", "tp"), None),
            P("rep", "tp"),
            P("rep", "tp"),
            P("rep", "tp"),
            P("rep", "tp"),
        ),
        out_specs=(P("rep", "tp"), P("rep", "tp"), P("rep", "tp"), P("rep", "tp"), P(None, "tp")),
        check_vma=False,
    )
```

profile of v0, /device:TPU:1, one launch (start us, length us, event | category | flops | bytes accessed | tf_op | source)
XLA Modules:
  0.0 306.9 jit_solution(14428147815570092287)
XLA Ops:
  8.0 128.0 %all-gather.3.cloned.1.call-done = bf16[4096,1024]{1,0:T(8,128)(2,1)} async-done(((bf16[512,1024]{1,0:T(8,128)(2,1)}), bf16[4096,1024]{1,0:T(8,128)(2,1)}) %all-gather.3.cloned.1.call-update) | async-done | bytes 8388624 | tf_op jit(solution)/shard_map/all_gather | solution.py:48
  136.0 8.2 %fusion.2 = f32[512,1024]{1,0:T(8,128)S(1)} fusion(bf16[4096,1024]{1,0:T(8,128)(2,1)} %param.6, bf16[4096,1024]{1,0:T(8,128)(2,1)} %all-gather.3.cloned.1.call-done, s32[]{:T(128)S(6)} %select_n.42), kind=kOutput, calls=%fused_computation.2 | convolution fusion | flops 4294967296 | bytes 14680068 | tf_op jit(solution)/shard_map/dot_general | solution.py:54
  144.2 1.3 collective-permute-start
  145.4 44.7 %collective-permute-done = f32[512,1024]{1,0:T(8,128)} collective-permute-done((f32[512,1024]{1,0:T(8,128)S(1)}, f32[512,1024]{1,0:T(8,128)}, u32[]{:S(2)}, u32[]{:S(2)}) %collective-permute-start) | collective-permute-done | bytes 2097184 | tf_op jit(solution)/shard_map/ppermute | solution.py:15
  190.1 11.9 %multiply_reduce_fusion.2 = (f32[]{:T(128)}, f32[]{:T(128)}, f32[]{:T(128)}, f32[512,1024]{1,0:T(8,128)S(1)}, f32[512,1024]{1,0:T(8,128)}) fusion(f32[512,1024]{1,0:T(8,128)} %collective-permute-done, pred[]{:T(512)S(6)} %eq.7, bf16[4096,1024]{1,0:T(8,128)(2,1)} %param.6, bf16[4096,1024]{1,0:T(8,128)(2,1)} %all-gather.3.cloned.1.call-done, s32[]{:T(128)S(6)} %select_n.43), kind=kOutput, calls=%fused_computation.7 | convolution fusion | flops 4299161600 | bytes 18874384 | tf_op jit(solution)/shard_map/dot_general | solution.py:59
  202.0 2.0 pad_maximum_fusion
  204.0 1.2 collective-permute-start.1
  205.2 1.2 collective-permute-done.1
  206.5 2.0 fusion.14
  208.5 16.4 %psum.14 = f32[3]{0:T(128)S(1)} all-reduce(f32[3]{0:T(128)S(1)} %fusion.14), channel_id=1, replica_groups=mesh['rep'=4,'tp'=8] {'tp'}, use_global_device_ids=true, to_apply=%region_3.4 | all-reduce | flops 3 | bytes 24 | tf_op jit(solution)/shard_map/psum | solution.py:34
  228.0 2.0 multiply_add_fusion
  230.2 6.4 %collective-permute-start.2 = (f32[256,1024]{1,0:T(8,128)S(1)}, f32[256,1024]{1,0:T(8,128)S(1)}, u32[]{:S(2)}, u32[]{:S(2)}) collective-permute-start(f32[256,1024]{1,0:T(8,128)S(1)} %slice_select_fusion.1), channel_id=1, source_target_pairs={{0,8},{8,0},{16,24},{24,16},{1,9},{9,1},{17,25},{25,17},{2,10},{10... | collective-permute-start | bytes 3145736 | tf_op jit(solution)/shard_map/ppermute | solution.py:15
  236.6 2.3 collective-permute-done.2
  238.9 1.3 multiply_reduce_fusion.5
  240.3 2.0 pad_maximum_fusion.1
  242.7 0.8 collective-permute-done.3
  243.5 2.0 fusion.13
  245.5 1.2 collective-permute-start.4
  246.7 1.2 collective-permute-done.4
  247.9 2.0 fusion.15
  249.9 13.7 %psum.15 = f32[3]{0:T(128)S(1)} all-reduce(f32[3]{0:T(128)S(1)} %fusion.15), channel_id=1, replica_groups=mesh['rep'=4,'tp'=8] {'tp'}, use_global_device_ids=true, to_apply=%region_7.8 | all-reduce | flops 3 | bytes 24 | tf_op jit(solution)/shard_map/psum | solution.py:34
  266.8 4.1 %fusion.7 = (bf16[256,1024]{1,0:T(8,128)(2,1)}, f32[256,1024]{1,0:T(8,128)}, f32[256,1024]{1,0:T(8,128)}, f32[256,1024]{1,0:T(8,128)}, f32[256,1024]{1,0:T(8,128)}) fusion(f32[256,1024]{1,0:T(8,128)S(1)} %copy-done, f32[256,1024]{1,0:T(8,128)} %param.9, f32[256,1024]{1,0:T(8,128)} %param.8, f32[256,1024]{1,0:T(8,128)S(1)} %get-tuple-element.17, f32[]{:T(128)} %bitcast.9, ...), kind=kLoop, calls=%fused_computation.26 | loop fusion | flops 4194304 | bytes 9961480 | tf_op jit(solution)/shard_map/convert_element_type | solution.py:79
  271.0 26.1 %all-gather.5.cloned.1.call-done = bf16[1024,1024]{1,0:T(8,128)(2,1)} async-done(((bf16[256,1024]{1,0:T(8,128)(2,1)}), bf16[1024,1024]{1,0:T(8,128)(2,1)}) %all-gather.5.cloned.1.call-update) | async-done | bytes 2097168 | tf_op jit(solution)/shard_map/all_gather | solution.py:79
  297.0 3.1 %copy.11 = bf16[1024,1024]{1,0:T(8,128)(2,1)} copy(bf16[1024,1024]{1,0:T(8,128)(2,1)} %all-gather.5.cloned.1.call-done) | data formatting | bytes 4194304
  (10 shorter events, 2.5 us)
Async XLA Ops:
  7.2 128.8 %all-gather.3.cloned.1.call-start = ((), (), s32[]{:S(2)}) async-start(), calls=%async_computation | async-start | bytes 9437184 | tf_op jit(solution)/shard_map/all_gather | solution.py:48
  7.9 289.1 %all-gather.5.cloned.1.call-start = ((), (), s32[]{:S(2)}) async-start(), calls=%async_computation.1 | async-start | bytes 2621440 | tf_op jit(solution)/shard_map/all_gather | solution.py:79
  144.2 46.0 %collective-permute-start = (f32[512,1024]{1,0:T(8,128)S(1)}, f32[512,1024]{1,0:T(8,128)}, u32[]{:S(2)}, u32[]{:S(2)}) collective-permute-start(f32[512,1024]{1,0:T(8,128)S(1)} %fusion.2), channel_id=1, source_target_pairs={{0,16},{8,24},{16,0},{24,8},{1,17},{9,25},{17,1},{25,9},{2,18},{10... | collective-permute-start | bytes 6291464 | tf_op jit(solution)/shard_map/ppermute | solution.py:15
  204.0 2.4 collective-permute-start.1
  230.2 36.6 %copy-start = (f32[256,1024]{1,0:T(8,128)S(1)}, f32[256,1024]{1,0:T(8,128)}, u32[]{:S(2)}) copy-start(f32[256,1024]{1,0:T(8,128)} %param.7) | copy-start | bytes 3145732
  230.2 8.7 %collective-permute-start.2 = (f32[256,1024]{1,0:T(8,128)S(1)}, f32[256,1024]{1,0:T(8,128)S(1)}, u32[]{:S(2)}, u32[]{:S(2)}) collective-permute-start(f32[256,1024]{1,0:T(8,128)S(1)} %slice_select_fusion.1), channel_id=1, source_target_pairs={{0,8},{8,0},{16,24},{24,16},{1,9},{9,1},{17,25},{25,17},{2,10},{10... | collective-permute-start | bytes 3145736 | tf_op jit(solution)/shard_map/ppermute | solution.py:15
  242.3 1.2 collective-permute-start.3
  245.5 2.4 collective-permute-start.4
Sparse Core Ops, SparseCore 0:
  10.1 125.8 all-gather.2
  271.1 25.9 all-gather.4
where the time goes:
time: 308 us; the launch traced here: 307 us
  waiting for transfers between devices  205 us (67%)
  blocking collectives  30 us (10%)
  matrix products  20.1 us (7%)
  between operations  19.3 us (6%)
  other arithmetic  17.7 us (6%)
  starting transfers between devices  10.5 us (3%)
  local copies, waits for them, and re-layouts  4.26 us (1%)
    all_gather x1, waiting for transfers between devices, per_device(): gathered_rows = lax.all_gather(inputs, 'tp', axis=0, tiled=True)  128 us
    ppermute x5, waiting for transfers between devices, from_partner(): lax.ppermute(value, axis, [(i, i ^ 1 << stride) for i in range(lax.axis_s...  50.2 us
    psum x2, blocking collectives, combine_level(): partial_value = lax.psum(partial_value, 'tp')  30 us
    all_gather x1, waiting for transfers between devices, per_device(): lax.all_gather(master_new.astype(jnp.bfloat16), 'rep', axis=0, tiled=True)  26.1 us
    dot_general x1, matrix products, per_device(): lax.dot_general(kept_columns, cotangent, (((0,), (0,)), ((), ())), prefer...  11.9 us
    ppermute x5, starting transfers between devices, from_partner(): lax.ppermute(value, axis, [(i, i ^ 1 << stride) for i in range(lax.axis_s...  10.5 us
    dot_general x1, matrix products, per_device(): lax.dot_general(sent_columns, cotangent, (((0,), (0,)), ((), ())), prefer...  8.2 us
  transfers between devices with their start and end apart: 7, of which 7 were waited for; matrix products, arithmetic and copies ran while one was open for 0% of the time, Pallas kernels for 0%

commit v1 on v0

v1 whole, which is shorter than its diff:
```python
import functools
import jax
import jax.numpy as jnp
from jax import lax
from jax.experimental import pallas as pl
from jax.experimental.pallas import tpu as pltpu
from jax.sharding import PartitionSpec as P

EPS_SUM = 1e-06
BETA_ONE = 0.9
BETA_TWO = 0.999
LEARN = 0.01
CORRECT_ONE = 1.0 - 0.9**50
CORRECT_TWO = 1.0 - 0.999**50
LANES = 128
SUBLANES = 8
PIECES = 4
OWN_LEAD = 2
MESH = pl.DeviceIdType.MESH


def adasum_weights(gram, replicas):
    entries = [{s: jnp.ones((1, 1), jnp.float32)} for s in range(replicas)]

    def inner(left, right):
        total = None
        for i, u in left.items():
            for j, v in right.items():
                term = (u * v) * gram[min(i, j), max(i, j)]
                total = term if total is None else total + term
        return total

    while len(entries) > 1:
        half = len(entries) // 2
        merged = []
        for a, b in zip(entries[:half], entries[half:]):
            aa, bb, ab = inner(a, a), inner(b, b), inner(a, b)
            ca = 1.0 - ab / (2.0 * (aa + EPS_SUM))
            cb = 1.0 - ab / (2.0 * (bb + EPS_SUM))
            merged.append({**{i: ca * u for i, u in a.items()}, **{i: cb * u for i, u in b.items()}})
        entries = merged
    return entries[0]


def kernel(
    replicas, outer, inner,
    x_hbm, g_hbm, master_hbm, moment_hbm, second_hbm,
    comb_hbm, mom_hbm, sec_hbm, mas_hbm, w_hbm,
    xg, cot, gsend, gr, master, moment, second, comb, mom, sec, mas, wb, tile_tp, tile_rep,
    load_x, load_g, load_s, x_send, x_recv, g_send, g_recv, t_send, t_recv, r_send, r_recv, w_send, w_recv, out_sem,
):
    rep = lax.axis_index("rep")
    tp = lax.axis_index("tp")
    peers = outer * inner
    i, j = tp // inner, tp % inner
    chunks = xg.shape[0]
    width = xg.shape[3]
    tokens = xg.shape[2]
    per_segment = chunks // replicas
    segment_order = list(range(replicas - 1, -1, -1))
    rows = gr.shape[1]

    loads = []
    for k in range(chunks):
        s, h = segment_order[k // per_segment], k % per_segment
        column = pl.multiple_of(((rep ^ s) * per_segment + h) * width, width)
        loads.append(pltpu.make_async_copy(x_hbm.at[:, pl.ds(column, width)], xg.at[k, tp], load_x.at[k]))
    for copy in loads:
        copy.start()
    load_cot = pltpu.make_async_copy(g_hbm, cot, load_g)
    load_cot.start()
    state_loads = [
        pltpu.make_async_copy(src, dst, load_s.at[n])
        for n, (src, dst) in enumerate(((master_hbm, master), (moment_hbm, moment), (second_hbm, second)))
    ]
    for copy in state_loads:
        copy.start()

    barrier = pltpu.get_barrier_semaphore()
    for d in range(1, peers):
        pl.semaphore_signal(barrier, inc=1, device_id=(rep, (tp + d) % peers), device_id_type=MESH)
    for s in range(1, replicas):
        pl.semaphore_signal(barrier, inc=1, device_id=(rep ^ s, tp), device_id_type=MESH)
    pl.semaphore_wait(barrier, peers - 1 + replicas - 1)

    pending = []

    def send(k, slot, direction, cond, to_i, to_j):
        target = jnp.clip(to_i, 0, outer - 1) * inner + jnp.clip(to_j, 0, inner - 1)
        copy = pltpu.make_async_remote_copy(
            xg.at[k, slot], xg.at[k, slot], x_send.at[k, direction, slot], x_recv.at[k, slot],
            device_id=(rep, target), device_id_type=MESH,
        )

        @pl.when(cond)
        def _():
            copy.start()

        pending.append((cond, copy))

    def wait_block(k, slot):
        pltpu.make_async_remote_copy(
            xg.at[k, slot], xg.at[k, slot], x_send.at[k, 0, slot], x_recv.at[k, slot],
            device_id=(rep, tp), device_id_type=MESH,
        ).wait_recv()

    def route(k):
        swap = k % 4 == 1
        if swap:
            n1, n2, p1, p2 = inner, outer, j, i
            slot_of = lambda q1, q2: q2 * inner + q1
            place = lambda q1, q2: (q2, q1)
        else:
            n1, n2, p1, p2 = outer, inner, i, j
            slot_of = lambda q1, q2: q1 * inner + q2
            place = lambda q1, q2: (q1, q2)
        return n1, n2, p1, p2, slot_of, place

    def cross(k, slot, cond, n2, p1, p2, place):
        up = p2 + 1 < n2
        down = p2 - 1 >= 0
        if cond is not None:
            up, down = cond & up, cond & down
        send(k, slot, 2, up, *place(p1, p2 + 1))
        send(k, slot, 3, down, *place(p1, p2 - 1))

    def own(k):
        n1, n2, p1, p2, slot_of, place = route(k)
        loads[k].wait()
        send(k, tp, 0, p1 + 1 < n1, *place(p1 + 1, p2))
        send(k, tp, 1, p1 - 1 >= 0, *place(p1 - 1, p2))
        cross(k, tp, None, n2, p1, p2, place)

    def first_line(k):
        n1, n2, p1, p2, slot_of, place = route(k)
        for t in range(1, n1):
            for step in (-1, 1):
                origin = p1 + step * t
                valid = (origin >= 0) & (origin < n1)
                slot = slot_of(jnp.clip(origin, 0, n1 - 1), p2)

                @pl.when(valid)
                def _():
                    wait_block(k, slot)

                onward = p1 - step
                send(k, slot, 0 if step < 0 else 1, valid & (onward >= 0) & (onward < n1), *place(onward, p2))
                cross(k, slot, valid, n2, p1, p2, place)

    def second_line(k):
        n1, n2, p1, p2, slot_of, place = route(k)
        for u in range(1, n2):
            for step in (-1, 1):
                origin = p2 + step * u
                valid = (origin >= 0) & (origin < n2)
                onward = p2 - step
                go = valid & (onward >= 0) & (onward < n2)
                for r in range(n1):
                    slot = slot_of((p1 + r) % n1, jnp.clip(origin, 0, n2 - 1))

                    @pl.when(valid)
                    def _():
                        wait_block(k, slot)

                    if n2 > 2:
                        send(k, slot, 2 if step < 0 else 3, go, *place(p1, onward))

    grad_sends = []

    def consume(k):
        s, h = segment_order[k // per_segment], k % per_segment
        at = pl.ds(h * width, width)
        target = gsend.at[s - 1, at] if s else gr.at[0, at]

        def accumulate(slot, carry):
            part = lax.dot_general(
                xg[k, slot], cot[pl.ds(pl.multiple_of(slot * tokens, tokens), tokens), :],
                (((0,), (0,)), ((), ())), preferred_element_type=jnp.float32,
            )
            target[...] = target[...] + part
            return carry

        target[...] = lax.dot_general(
            xg[k, 0], cot[pl.ds(0, tokens), :], (((0,), (0,)), ((), ())), preferred_element_type=jnp.float32
        )
        lax.fori_loop(1, peers, accumulate, 0)
        if s:
            copy = pltpu.make_async_remote_copy(
                gsend.at[s - 1, at], gr.at[s, at], g_send.at[s - 1, h], g_recv.at[s - 1, h],
                device_id=(rep ^ s, tp), device_id_type=MESH,
            )
            copy.start()
            grad_sends.append(copy)

    for k in range(min(OWN_LEAD, chunks)):
        own(k)
    first_line(0)
    load_cot.wait()
    for k in range(chunks):
        if k + OWN_LEAD < chunks:
            own(k + OWN_LEAD)
        if k + 1 < chunks:
            first_line(k + 1)
        second_line(k)
        consume(k)
    for copy in grad_sends:
        copy.wait_recv()

    pairs = [(s, t) for s in range(replicas) for t in range(s, replicas)]
    fold = gr.shape[2] // LANES

    def products(n, sums):
        block = [gr[s, pl.ds(pl.multiple_of(n * SUBLANES, SUBLANES), SUBLANES), :] for s in range(replicas)]
        out = []
        for total, (s, t) in zip(sums, pairs):
            prod = block[s] * block[t]
            part = prod[:, :LANES]
            for f in range(1, fold):
                part = part + prod[:, f * LANES : (f + 1) * LANES]
            out.append(total + part)
        return tuple(out)

    sums = lax.fori_loop(
        0, rows // SUBLANES, products, tuple(jnp.zeros((SUBLANES, LANES), jnp.float32) for _ in pairs)
    )
    lane = lax.broadcasted_iota(jnp.int32, (SUBLANES, LANES), 1)
    packed = jnp.zeros((SUBLANES, LANES), jnp.float32)
    for n, total in enumerate(sums):
        packed = jnp.where(lane == n, jnp.sum(total, axis=1, keepdims=True), packed)
    tile_tp[0] = packed
    tile_sends = []
    for d in range(1, peers):
        copy = pltpu.make_async_remote_copy(
            tile_tp.at[0], tile_tp.at[d], t_send.at[d - 1], t_recv.at[d - 1],
            device_id=(rep, (tp + d) % peers), device_id_type=MESH,
        )
        copy.start()
        tile_sends.append(copy)
    for copy in state_loads:
        copy.wait()
    for copy in tile_sends:
        copy.wait_recv()
    packed = tile_tp[0]
    for d in range(1, peers):
        packed = packed + tile_tp[d]
    tile_rep[0] = packed
    for s in range(1, replicas):
        copy = pltpu.make_async_remote_copy(
            tile_rep.at[0], tile_rep.at[s], r_send.at[s - 1], r_recv.at[s - 1],
            device_id=(rep ^ s, tp), device_id_type=MESH,
        )
        copy.start()
        tile_sends.append(copy)
    for copy in tile_sends[peers - 1 :]:
        copy.wait_recv()
    index = {pair: n for n, pair in enumerate(pairs)}
    seen = [tile_rep[s] for s in range(replicas)]
    gram = {}
    for s, t in pairs:
        value = None
        for d in range(replicas):
            p, q = s ^ d, t ^ d
            picked = jnp.where(lane == index[min(p, q), max(p, q)], seen[d], 0.0)
            value = picked if value is None else value + picked
        gram[s, t] = jnp.sum(value, keepdims=True)
    coef = adasum_weights(gram, replicas)
    coef = [jnp.broadcast_to(coef[s], (SUBLANES, gr.shape[2])) for s in range(replicas)]

    masks = []
    mask = replicas // 2
    while mask:
        masks.append(mask)
        mask //= 2
    piece = rows // PIECES
    outs = []
    w_copies = {}

    def w_send_start(step, s, q):
        m = masks[step]
        at = pl.ds(q * piece, piece)
        copy = pltpu.make_async_remote_copy(
            wb.at[s, at], wb.at[s ^ m, at], w_send.at[s ^ m, q], w_recv.at[s ^ m, q],
            device_id=(rep ^ m, tp), device_id_type=MESH,
        )
        copy.start()
        w_copies[s ^ m, q] = copy

    def put(src, dst, n):
        copy = pltpu.make_async_copy(src, dst, out_sem.at[n])
        copy.start()
        outs.append(copy)

    for q in range(PIECES):
        def update(n, carry):
            at = pl.ds(pl.multiple_of(q * piece + n * SUBLANES * 2, SUBLANES * 2), SUBLANES * 2)
            value = None
            for s in range(replicas):
                term = coef[s][:1] * gr[s, at, :]
                value = term if value is None else value + term
            moment_new = BETA_ONE * moment[at, :] + (1.0 - BETA_ONE) * value
            second_new = BETA_TWO * second[at, :] + (1.0 - BETA_TWO) * value * value
            master_new = master[at, :] - LEARN * (moment_new / CORRECT_ONE) / (
                jnp.sqrt(second_new / CORRECT_TWO) + 1e-08
            )
            comb[at, :] = value
            mom[at, :] = moment_new
            sec[at, :] = second_new
            mas[at, :] = master_new
            wb[0, at, :] = master_new.astype(jnp.bfloat16)
            return carry

        lax.fori_loop(0, piece // (SUBLANES * 2), update, 0)
        for step in range(len(masks)):
            w_send_start(step, 0, q)
    for n, (src, dst) in enumerate(((comb, comb_hbm), (mom, mom_hbm), (sec, sec_hbm), (mas, mas_hbm))):
        put(src, dst, n)
    put(wb.at[0], w_hbm.at[pl.ds(pl.multiple_of(rep * rows, rows), rows)], 4)

    def relay(q, step, s):
        w_copies[s, q].wait_recv()
        for later in range(step + 1, len(masks)):
            w_send_start(later, s, q)

    held = [0]
    for step, m in enumerate(masks):
        fresh = [s ^ m for s in held]
        for q in range(PIECES):
            for s in fresh:
                relay(q, step, s)
        for s in fresh:
            put(wb.at[s], w_hbm.at[pl.ds(pl.multiple_of((rep ^ s) * rows, rows), rows)], 4 + s)
        held = held + fresh

    for cond, copy in pending:
        @pl.when(cond)
        def _():
            copy.wait_send()
    for copy in grad_sends + tile_sends + list(w_copies.values()):
        copy.wait_send()
    for copy in outs:
        copy.wait()


def per_device(inputs, cotangent, master, moment, second):
    replicas = lax.axis_size("rep")
    peers = lax.axis_size("tp")
    inner = 1 << (peers.bit_length() - 1) // 2
    outer = peers // inner
    tokens, depth = inputs.shape
    features = cotangent.shape[1]
    rows = depth // replicas
    width = min(LANES, rows)
    chunks = depth // width
    per_segment = rows // width
    shard = jax.ShapeDtypeStruct((rows, features), jnp.float32)
    anywhere = pl.BlockSpec(memory_space=pl.ANY)
    dma = pltpu.SemaphoreType.DMA
    small = pltpu.VMEM((rows, features), jnp.float32)
    return pl.pallas_call(
        functools.partial(kernel, replicas, outer, inner),
        out_shape=(shard, shard, shard, shard, jax.ShapeDtypeStruct((depth, features), jnp.bfloat16)),
        in_specs=[anywhere] * 5,
        out_specs=(anywhere,) * 5,
        scratch_shapes=[
            pltpu.VMEM((chunks, peers, tokens, width), jnp.bfloat16),
            pltpu.VMEM(cotangent.shape, jnp.bfloat16),
            pltpu.VMEM((replicas - 1, rows, features), jnp.float32),
            pltpu.VMEM((replicas, rows, features), jnp.float32),
            small, small, small, small, small, small, small,
            pltpu.VMEM((replicas, rows, features), jnp.bfloat16),
            pltpu.VMEM((peers, SUBLANES, LANES), jnp.float32),
            pltpu.VMEM((replicas, SUBLANES, LANES), jnp.float32),
            dma((chunks,)),
            dma,
            dma((3,)),
            dma((chunks, 4, peers)),
            dma((chunks, peers)),
            dma((replicas - 1, per_segment)),
            dma((replicas - 1, per_segment)),
            dma((peers - 1,)),
            dma((peers - 1,)),
            dma((replicas - 1,)),
            dma((replicas - 1,)),
            dma((replicas, PIECES)),
            dma((replicas, PIECES)),
            dma((4 + replicas,)),
        ],
        compiler_params=pltpu.CompilerParams(
            collective_id=0, has_side_effects=True, vmem_limit_bytes=60 * 1024 * 1024
        ),
        name="adasum_adam",
    )(inputs, cotangent, master, moment, second)


def solution(mesh):
    return jax.shard_map(
        per_device,
        mesh=mesh,
        in_specs=(
            P(("rep", "tp"), None),
            P("rep", "tp"),
            P("rep", "tp"),
            P("rep", "tp"),
            P("rep", "tp"),
        ),
        out_specs=(P("rep", "tp"), P("rep", "tp"), P("rep", "tp"), P("rep", "tp"), P(None, "tp")),
        check_vma=False,
    )
```

time: 308 us -> 137 us (0.44)
  waiting for transfers between devices: 205 us -> 0 us
  Pallas kernels: 0 us -> 129 us
  blocking collectives: 30 us -> 0 us
  matrix products: 20.1 us -> 0 us
  between operations: 19.3 us -> 0.66 us
  other arithmetic: 17.7 us -> 0 us
  starting transfers between devices: 10.5 us -> 0 us
    all_gather x2 -> x0, waiting for transfers between devices: 154 us -> none  [the longest x1 128 us: per_device(): gathered_rows = lax.all_gather(inputs, 'tp', axis=0, tiled=True)]
    pallas_call x0 -> x1, Pallas kernels: none -> 129 us  [per_device(): pl.pallas_call(functools.partial(kernel, replicas, outer, inner), out_sha...]
    ppermute x5 -> x0, waiting for transfers between devices: 50.2 us -> none  [from_partner(): lax.ppermute(value, axis, [(i, i ^ 1 << stride) for i in range(lax.axis_s...]
    psum x2 -> x0, blocking collectives: 30 us -> none  [combine_level(): partial_value = lax.psum(partial_value, 'tp')]
    dot_general x2 -> x0, matrix products: 20.1 us -> none  [the longest x1 11.9 us: per_device(): lax.dot_general(kept_columns, cotangent, (((0,), (0,)), ((), ())), prefer...]
    ppermute x5 -> x0, starting transfers between devices: 10.5 us -> none  [from_partner(): lax.ppermute(value, axis, [(i, i ^ 1 << stride) for i in range(lax.axis_s...]
    add x4 -> x0, other arithmetic: 8.08 us -> none  [the longest x3 6.04 us: combine_level(): partial_value + from_partner(partial_value, 'rep', inner_bit)]
    convert_element_type x1 -> x0, other arithmetic: 4.13 us -> none  [per_device(): master_new.astype(jnp.bfloat16)]
  transfers between devices with their start and end apart: 7 -> 0, of which waited for: 7 -> 0; matrix products, arithmetic and copies ran while one was open for 0% -> 0% of each run, Pallas kernels for 0% -> 0%
where the time goes in v1:
time: 137 us
  Pallas kernels  129 us (94%)
  local copies, waits for them, and re-layouts  6.85 us (5%)
    pallas_call x1, Pallas kernels, per_device(): pl.pallas_call(functools.partial(kernel, replicas, outer, inner), out_sha...  129 us
    unnamed x13, local copies, waits for them, and re-layouts  6.85 us

profile of v1, /device:TPU:1, one launch (start us, length us, event | category | flops | bytes accessed | tf_op | source)
XLA Modules:
  0.0 136.9 jit_solution(6565191101101722525)
XLA Ops:
  0.6 129.4 %adasum_adam.1 = (f32[256,1024]{1,0:T(8,128)}, f32[256,1024]{1,0:T(8,128)}, f32[256,1024]{1,0:T(8,128)}, f32[256,1024]{1,0:T(8,128)}, bf16[1024,1024]{1,0:T(8,128)(2,1)}) custom-call(bf16[512,1024]{1,0:T(8,128)(2,1)} %x_hbm.1, bf16[4096,1024]{1,0:T(8,128)(2,1)} %g_hbm.1, f32[256,1024]{1,0:T(8,128)} %master_hbm.1, f32[256,1024]{1,0:T(8,128)} %moment_hbm.1, ...), custom_call_target="tpu_custom_call" | custom-call | tf_op jit(solution)/shard_map/adasum_adam/pallas_call | solution.py:359
  130.1 0.0 copy-start.3
  130.1 0.0 copy-start.2
  130.1 2.5 %copy.15 = f32[256,1024]{1,0:T(8,128)} copy(f32[256,1024]{1,0:T(8,128)} %get-tuple-element.10) | data formatting | bytes 2097152
  132.5 0.0 copy-done.3
  132.6 0.0 copy-start.1
  132.6 1.0 copy.16
  133.5 0.0 copy-done.2
  133.5 0.0 copy-start
  133.5 1.0 copy.17
  134.5 0.0 copy-done.1
  134.5 1.0 copy.18
  135.5 0.1 copy-done
  135.6 1.3 copy.19
Async XLA Ops:
  130.1 2.5 %copy-start.3 = (f32[256,1024]{1,0:T(8,128)S(1)}, f32[256,1024]{1,0:T(8,128)}, u32[]{:S(2)}) copy-start(f32[256,1024]{1,0:T(8,128)} %get-tuple-element.11) | copy-start | bytes 3145732
  130.1 3.4 %copy-start.2 = (f32[256,1024]{1,0:T(8,128)S(1)}, f32[256,1024]{1,0:T(8,128)}, u32[]{:S(2)}) copy-start(f32[256,1024]{1,0:T(8,128)} %get-tuple-element.12) | copy-start | bytes 3145732
  132.6 1.9 %copy-start.1 = (f32[256,1024]{1,0:T(8,128)S(1)}, f32[256,1024]{1,0:T(8,128)}, u32[]{:S(2)}) copy-start(f32[256,1024]{1,0:T(8,128)} %get-tuple-element.13) | copy-start | bytes 3145732
  133.5 2.1 %copy-start = (bf16[1024,1024]{1,0:T(8,128)(2,1)S(1)}, bf16[1024,1024]{1,0:T(8,128)(2,1)}, u32[]{:S(2)}) copy-start(bf16[1024,1024]{1,0:T(8,128)(2,1)} %get-tuple-element.14) | copy-start | bytes 6291460

commit v2 on v1

--- a/solution.py
+++ b/solution.py
@@ -15,7 +15,10 @@
 LANES = 128
 SUBLANES = 8
 PIECES = 4
-OWN_LEAD = 2
+SPLIT = 2
+OWN_LEAD = 9
+LINE_LEAD = 6
+INNER_FIRST = 5
 MESH = pl.DeviceIdType.MESH
 
 
@@ -53,22 +56,30 @@
     tp = lax.axis_index("tp")
     peers = outer * inner
     i, j = tp // inner, tp % inner
-    chunks = xg.shape[0]
+    units = xg.shape[0]
     width = xg.shape[3]
     tokens = xg.shape[2]
+    chunks = units // SPLIT
     per_segment = chunks // replicas
     segment_order = list(range(replicas - 1, -1, -1))
     rows = gr.shape[1]
 
     loads = []
-    for k in range(chunks):
-        s, h = segment_order[k // per_segment], k % per_segment
+    for k in range(units):
+        c, part = k // SPLIT, k % SPLIT
+        s, h = segment_order[c // per_segment], c % per_segment
         column = pl.multiple_of(((rep ^ s) * per_segment + h) * width, width)
-        loads.append(pltpu.make_async_copy(x_hbm.at[:, pl.ds(column, width)], xg.at[k, tp], load_x.at[k]))
+        source = x_hbm.at[pl.ds(part * tokens, tokens), pl.ds(column, width)]
+        loads.append(pltpu.make_async_copy(source, xg.at[k, tp], load_x.at[k]))
     for copy in loads:
         copy.start()
-    load_cot = pltpu.make_async_copy(g_hbm, cot, load_g)
-    load_cot.start()
+    cot_loads = []
+    for part in range(SPLIT):
+        for slot in range(peers):
+            source = g_hbm.at[pl.ds((slot * SPLIT + part) * tokens, tokens)]
+            cot_loads.append(pltpu.make_async_copy(source, cot.at[part, pl.ds(slot * tokens, tokens)], load_g.at[part, slot]))
+    for copy in cot_loads:
+        copy.start()
     state_loads = [
         pltpu.make_async_copy(src, dst, load_s.at[n])
         for n, (src, dst) in enumerate(((master_hbm, master), (moment_hbm, moment), (second_hbm, second)))
@@ -105,7 +116,7 @@
         ).wait_recv()
 
     def route(k):
-        swap = k % 4 == 1
+        swap = k % INNER_FIRST == 1
         if swap:
             n1, n2, p1, p2 = inner, outer, j, i
             slot_of = lambda q1, q2: q2 * inner + q1
@@ -168,61 +179,64 @@
     grad_sends = []
 
     def consume(k):
-        s, h = segment_order[k // per_segment], k % per_segment
+        c, part = k // SPLIT, k % SPLIT
+        s, h = segment_order[c // per_segment], c % per_segment
         at = pl.ds(h * width, width)
         target = gsend.at[s - 1, at] if s else gr.at[0, at]
-
-        def accumulate(slot, carry):
-            part = lax.dot_general(
-                xg[k, slot], cot[pl.ds(pl.multiple_of(slot * tokens, tokens), tokens), :],
-                (((0,), (0,)), ((), ())), preferred_element_type=jnp.float32,
-            )
-            target[...] = target[...] + part
-            return carry
-
-        target[...] = lax.dot_general(
-            xg[k, 0], cot[pl.ds(0, tokens), :], (((0,), (0,)), ((), ())), preferred_element_type=jnp.float32
+        product = lax.dot_general(
+            xg[k].reshape(peers * tokens, width), cot[part],
+            (((0,), (0,)), ((), ())), preferred_element_type=jnp.float32,
         )
-        lax.fori_loop(1, peers, accumulate, 0)
-        if s:
+        target[...] = target[...] + product if part else product
+        if s and part == SPLIT - 1:
             copy = pltpu.make_async_remote_copy(
                 gsend.at[s - 1, at], gr.at[s, at], g_send.at[s - 1, h], g_recv.at[s - 1, h],
                 device_id=(rep ^ s, tp), device_id_type=MESH,
             )
             copy.start()
-            grad_sends.append(copy)
-
-    for k in range(min(OWN_LEAD, chunks)):
-        own(k)
-    first_line(0)
-    load_cot.wait()
-    for k in range(chunks):
-        if k + OWN_LEAD < chunks:
-            own(k + OWN_LEAD)
-        if k + 1 < chunks:
-            first_line(k + 1)
-        second_line(k)
-        consume(k)
-    for copy in grad_sends:
-        copy.wait_recv()
+            grad_sends.append((h, copy))
 
     pairs = [(s, t) for s in range(replicas) for t in range(s, replicas)]
     fold = gr.shape[2] // LANES
 
-    def products(n, sums):
-        block = [gr[s, pl.ds(pl.multiple_of(n * SUBLANES, SUBLANES), SUBLANES), :] for s in range(replicas)]
-        out = []
-        for total, (s, t) in zip(sums, pairs):
-            prod = block[s] * block[t]
-            part = prod[:, :LANES]
-            for f in range(1, fold):
-                part = part + prod[:, f * LANES : (f + 1) * LANES]
-            out.append(total + part)
-        return tuple(out)
-
-    sums = lax.fori_loop(
-        0, rows // SUBLANES, products, tuple(jnp.zeros((SUBLANES, LANES), jnp.float32) for _ in pairs)
-    )
+    def inner_products(h, sums):
+        for at_h, copy in grad_sends:
+            if at_h == h:
+                copy.wait_recv()
+
+        def products(n, sums):
+            at = pl.ds(pl.multiple_of(h * width + n * SUBLANES, SUBLANES), SUBLANES)
+            block = [gr[s, at, :] for s in range(replicas)]
+            out = []
+            for total, (s, t) in zip(sums, pairs):
+                prod = block[s] * block[t]
+                part = prod[:, :LANES]
+                for f in range(1, fold):
+                    part = part + prod[:, f * LANES : (f + 1) * LANES]
+                out.append(total + part)
+            return tuple(out)
+
+        return lax.fori_loop(0, width // SUBLANES, products, sums)
+
+    sums = tuple(jnp.zeros((SUBLANES, LANES), jnp.float32) for _ in pairs)
+    for k in range(min(OWN_LEAD, units)):
+        own(k)
+    for k in range(min(LINE_LEAD, units)):
+        first_line(k)
+    for copy in cot_loads:
+        copy.wait()
+    for k in range(units):
+        if k + OWN_LEAD < units:
+            own(k + OWN_LEAD)
+        if k + LINE_LEAD < units:
+            first_line(k + LINE_LEAD)
+        second_line(k)
+        if k == units - 1:
+            for h in range(per_segment - 1):
+                sums = inner_products(h, sums)
+        consume(k)
+    sums = inner_products(per_segment - 1, sums)
+    seg_sends = [copy for _, copy in grad_sends]
     lane = lax.broadcasted_iota(jnp.int32, (SUBLANES, LANES), 1)
     packed = jnp.zeros((SUBLANES, LANES), jnp.float32)
     for n, total in enumerate(sums):
@@ -335,10 +349,27 @@
         @pl.when(cond)
         def _():
             copy.wait_send()
-    for copy in grad_sends + tile_sends + list(w_copies.values()):
+    for copy in seg_sends + tile_sends + list(w_copies.values()):
         copy.wait_send()
     for copy in outs:
         copy.wait()
+
+
+def deliver(*refs):
+    sources, targets, buffers, (in_sem, out_sem) = refs[:5], refs[5:10], refs[10:15], refs[15:]
+    moves = []
+    for n, (src, dst, buf) in enumerate(zip(sources, targets, buffers)):
+        step = buf.shape[0] // PIECES
+        for q in range(PIECES):
+            at = pl.ds(q * step, step)
+            load = pltpu.make_async_copy(src.at[at], buf.at[at], in_sem.at[n, q])
+            load.start()
+            moves.append((load, pltpu.make_async_copy(buf.at[at], dst.at[at], out_sem.at[n, q])))
+    for load, store in moves:
+        load.wait()
+        store.start()
+    for _, store in moves:
+        store.wait()
 
 
 def per_device(inputs, cotangent, master, moment, second):
@@ -356,25 +387,25 @@
     anywhere = pl.BlockSpec(memory_space=pl.ANY)
     dma = pltpu.SemaphoreType.DMA
     small = pltpu.VMEM((rows, features), jnp.float32)
-    return pl.pallas_call(
+    results = pl.pallas_call(
         functools.partial(kernel, replicas, outer, inner),
         out_shape=(shard, shard, shard, shard, jax.ShapeDtypeStruct((depth, features), jnp.bfloat16)),
         in_specs=[anywhere] * 5,
         out_specs=(anywhere,) * 5,
         scratch_shapes=[
-            pltpu.VMEM((chunks, peers, tokens, width), jnp.bfloat16),
-            pltpu.VMEM(cotangent.shape, jnp.bfloat16),
+            pltpu.VMEM((chunks * SPLIT, peers, tokens // SPLIT, width), jnp.bfloat16),
+            pltpu.VMEM((SPLIT, cotangent.shape[0] // SPLIT, features), jnp.bfloat16),
             pltpu.VMEM((replicas - 1, rows, features), jnp.float32),
             pltpu.VMEM((replicas, rows, features), jnp.float32),
             small, small, small, small, small, small, small,
             pltpu.VMEM((replicas, rows, features), jnp.bfloat16),
             pltpu.VMEM((peers, SUBLANES, LANES), jnp.float32),
             pltpu.VMEM((replicas, SUBLANES, LANES), jnp.float32),
-            dma((chunks,)),
-            dma,
+            dma((chunks * SPLIT,)),
+            dma((SPLIT, peers)),
             dma((3,)),
-            dma((chunks, 4, peers)),
-            dma((chunks, peers)),
+            dma((chunks * SPLIT, 4, peers)),
+            dma((chunks * SPLIT, peers)),
             dma((replicas - 1, per_segment)),
             dma((replicas - 1, per_segment)),
             dma((peers - 1,)),
@@ -390,6 +421,15 @@
         ),
         name="adasum_adam",
     )(inputs, cotangent, master, moment, second)
+    return pl.pallas_call(
+        deliver,
+        out_shape=tuple(jax.ShapeDtypeStruct(r.shape, r.dtype) for r in results),
+        in_specs=[anywhere] * 5,
+        out_specs=(anywhere,) * 5,
+        scratch_shapes=[pltpu.VMEM(r.shape, r.dtype) for r in results] + [dma((5, PIECES)), dma((5, PIECES))],
+        compiler_params=pltpu.CompilerParams(vmem_limit_bytes=60 * 1024 * 1024),
+        name="deliver",
+    )(*results)
 
 
 def solution(mesh):

time: 137 us -> 135 us (0.985)
  local copies, waits for them, and re-layouts: 6.85 us -> 0 us
  Pallas kernels: 129 us -> 134 us
    unnamed x13 -> x0, local copies, waits for them, and re-layouts: 6.85 us -> none
    pallas_call x0 -> x1, Pallas kernels: none -> 5.44 us  [per_device(): pl.pallas_call(deliver, out_shape=tuple((jax.ShapeDtypeStruct(r.shape, r....]
where the time goes in v2:
time: 135 us; the launch traced here: 134 us
  Pallas kernels  134 us (99%)
    pallas_call x1, Pallas kernels, per_device(): pl.pallas_call(functools.partial(kernel, replicas, outer, inner), out_sha...  128 us
    pallas_call x1, Pallas kernels, per_device(): pl.pallas_call(deliver, out_shape=tuple((jax.ShapeDtypeStruct(r.shape, r....  5.44 us

profile of v2, /device:TPU:1, one launch (start us, length us, event | category | flops | bytes accessed | tf_op | source)
XLA Modules:
  0.0 134.4 jit_solution(2541834103547685560)
XLA Ops:
  0.6 128.2 %adasum_adam.1 = (f32[256,1024]{1,0:T(8,128)}, f32[256,1024]{1,0:T(8,128)}, f32[256,1024]{1,0:T(8,128)}, f32[256,1024]{1,0:T(8,128)}, bf16[1024,1024]{1,0:T(8,128)(2,1)}) custom-call(bf16[512,1024]{1,0:T(8,128)(2,1)} %x_hbm.1, bf16[4096,1024]{1,0:T(8,128)(2,1)} %g_hbm.1, f32[256,1024]{1,0:T(8,128)} %master_hbm.1, f32[256,1024]{1,0:T(8,128)} %moment_hbm.1, ...), custom_call_target="tpu_custom_call" | custom-call | tf_op jit(solution)/shard_map/adasum_adam/pallas_call | solution.py:390
  128.8 5.4 %deliver.1 = (f32[256,1024]{1,0:T(8,128)}, f32[256,1024]{1,0:T(8,128)}, f32[256,1024]{1,0:T(8,128)}, f32[256,1024]{1,0:T(8,128)}, bf16[1024,1024]{1,0:T(8,128)(2,1)}) custom-call(f32[256,1024]{1,0:T(8,128)} %get-tuple-element.10.refs_0_, f32[256,1024]{1,0:T(8,128)} %get-tuple-element.11.refs_1_, f32[256,1024]{1,0:T(8,128)} %get-tuple-element.12.refs_2_, ...), custom_call_target="tpu_custom_call" | custom-call | tf_op jit(solution)/shard_map/deliver/pallas_call | solution.py:424
